TPU v7x, 256 devices: a whole 4x4x8 slice. The times are simulated.
256 devices in a mesh: ctx: 16 (over y_lo, x, core), chan: 16 (over z, y_hi).
Axes of the slice: x: 4, y: 4 (y_hi: 2, y_lo: 2; y = y_hi * 2 + y_lo), z: 8, core: 2. Of those that a mesh axis runs over, the one named last changes fastest.
Arguments:
- features: bfloat16 [3, 4096, 4096], P(None, 'ctx', 'chan'), may hold values from -6 to 6
- saved_conv: bfloat16 [4096, 4096], P('ctx', 'chan'), may hold values from -6 to 6
- grad_out: bfloat16 [4096, 4096], P('ctx', 'chan'), may hold values from -6 to 6
- out_weight: bfloat16 [4096, 4096], P('chan'), may hold values from -0.09375 to 0.09375
- in_weight: bfloat16 [3, 4096, 4096], P(None, None, 'chan'), may hold values from -0.09375 to 0.09375
- short_taps: float32 [3, 3, 4096], P(None, None, 'chan'), may hold values from -3.5 to 3.5
- residues: float32 [16, 4096], P(None, 'chan'), may hold values from -1 to 1
- decay_time: float32 [16, 4096], P(None, 'chan'), may hold values from 25 to 20480
Outputs:
- grad_input: bfloat16 [4096, 4096], P('chan', 'ctx')
- grad_residue: float32 [16, 4096], P(None, 'chan')
All inputs are finite; a program needn't handle non-finite values.
Results may differ from a plain program's by a relative error of at most 0.019.
Values may be sent and summed in bfloat16 or wider, within the bound.
A program may use at most 64 MiB of HBM per device.

v0:
```python
import jax
import jax.numpy as jnp
from jax import lax
from jax.sharding import PartitionSpec as P


def passed_along(value, axis, steps):
    count = lax.axis_size(axis)
    leading, last = (max(0, -steps), min(count, count - steps))
    return lax.ppermute(value, axis, [(source, source + steps) for source in range(leading, last)])


def local(features, saved_conv, grad_out, out_weight, in_weight, short_taps, residues, decay_time):
    highest = lax.Precision.HIGHEST
    length = features.shape[1]
    width = features.shape[2]
    poles = residues.shape[0]
    taps = short_taps.shape[1]
    span_rows = 128
    blocks = length // span_rows
    query_act = features[0].astype(jnp.float32)
    key_act = features[1].astype(jnp.float32)
    value_act = features[2].astype(jnp.float32)
    contract = (((1,), (1,)), ((), ()))
    everything = lax.all_gather(grad_out, "chan", axis=1, tiled=True)
    grad_gate = lax.dot_general(
        everything, out_weight, contract, preferred_element_type=jnp.float32
    )
    grad_conv = grad_gate * query_act
    grad_query = grad_gate * saved_conv.astype(jnp.float32)
    product = key_act * value_act
    rate = 1.0 / decay_time
    offset = jnp.arange(span_rows, dtype=jnp.float32)
    falling = jnp.exp(-rate[None] * offset[:, None, None])
    rising = jnp.exp(rate[None] * offset[:, None, None])
    closing = jnp.exp(-rate[None] * (span_rows - offset)[:, None, None])
    weighted = grad_conv.reshape(blocks, span_rows, 1, width) * falling[None]
    upper = (offset[None, :] >= offset[:, None]).astype(jnp.float32)
    tails = jnp.einsum(
        "st,btx->bsx",
        upper,
        weighted.reshape(blocks, span_rows, poles * width),
        precision=highest,
        preferred_element_type=jnp.float32,
    )
    tails = tails.reshape(blocks, span_rows, poles, width)
    starts = tails[:, 0]
    order = jnp.arange(blocks)
    gap = order[None, :] - order[:, None] - 1
    distance = (span_rows * jnp.maximum(gap, 0)).astype(jnp.float32)
    factor = jnp.where(
        gap[:, :, None, None] >= 0, jnp.exp(-rate[None, None] * distance[:, :, None, None]), 0.0
    )
    beyond = jnp.sum(factor * starts[None], axis=1)
    block_span = jnp.exp(-rate * span_rows)
    own_start = starts[0] + block_span * beyond[0]
    device_span = jnp.exp(-rate * length)
    empty = jnp.zeros_like(rate)

    def relay(step, incoming):
        return passed_along(own_start + device_span * incoming, "ctx", -1)

    incoming = lax.fori_loop(0, lax.axis_size("ctx") - 1, relay, empty)
    remain = (blocks - 1 - order).astype(jnp.float32)
    entering = beyond + jnp.exp(-rate[None] * span_rows * remain[:, None, None]) * incoming[None]
    state = tails * rising[None] + closing[None] * entering[:, None]
    grad_product = jnp.sum(residues[None, None] * state, axis=2).reshape(length, width)
    partial_res = jnp.sum(product.reshape(blocks, span_rows, 1, width) * state, axis=(0, 1))
    grad_key = grad_product * value_act
    grad_value = grad_product * key_act
    grad_acts = jnp.stack([grad_query, grad_key, grad_value])
    after = passed_along(grad_acts[:, : taps - 1, :], "ctx", -1)
    extended = jnp.concatenate([grad_acts, after], axis=1)
    filtered = short_taps[:, 0, None, :] * extended[:, 0:length, :]
    for lag in range(1, taps):
        filtered = filtered + short_taps[:, lag, None, :] * extended[:, lag : lag + length, :]
    grad_proj = filtered.astype(jnp.bfloat16)
    grad_input = lax.psum_scatter(
        jnp.einsum("jdc,jtc->dt", in_weight, grad_proj, preferred_element_type=jnp.float32).astype(
            jnp.bfloat16
        ),
        "chan",
        scatter_dimension=0,
        tiled=True,
    )
    grad_residue = lax.psum(partial_res, "ctx") / (length * lax.axis_size("ctx"))
    return (grad_input, grad_residue)


def solution(mesh):
    return jax.shard_map(
        local,
        mesh=mesh,
        in_specs=(
            P(None, "ctx", "chan"),
            P("ctx", "chan"),
            P("ctx", "chan"),
            P("chan", None),
            P(None, None, "chan"),
            P(None, None, "chan"),
            P(None, "chan"),
            P(None, "chan"),
        ),
        out_specs=(P("chan", "ctx"), P(None, "chan")),
        check_vma=False,
    )
```

profile of v0, /device:TPU:2, one launch (start us, length us, event | category | flops | bytes accessed | tf_op | source)
XLA Modules:
  0.0 450.4 jit_solution(12016435469168271515)
XLA Ops:
  9.6 3.1 multiply_exponential_fusion.2
  12.7 2.3 multiply_exponential_fusion
  15.1 83.0 %all-gather.2.cloned.1.call-done = bf16[256,4096]{1,0:T(8,128)(2,1)} async-done(((bf16[256,256]{1,0:T(8,128)(2,1)}), bf16[256,4096]{1,0:T(8,128)(2,1)}) %all-gather.2.cloned.1.call-update) | async-done | bytes 2097168 | tf_op jit(solution)/shard_map/all_gather | solution.py:25
  98.1 2.3 multiply_bitcast_fusion
  102.4 2.1 fusion.12
  107.2 2.8 copy.34
  110.0 2.2 copy.35
  112.4 85.7 %while.10 = (s32[]{:T(128)}, f32[16,256]{1,0:T(8,128)S(1)}, f32[16,256]{1,0:T(8,128)S(1)}, f32[16,256]{1,0:T(8,128)S(1)}, s32[]{:T(128)}) while((s32[]{:T(128)}, f32[16,256]{1,0:T(8,128)S(1)}, f32[16,256]{1,0:T(8,128)S(1)}, f32[16,256]{1,0:T(8,128)S(1)}, s32[]{:T(128)}) %tuple.40), condition=%wide.region_2.3_spmd, body=%wide.region_1.2_spmd.sunk | while | flops 8194 | bytes 131173 | solution.py:63
  112.4 1.9 collective-permute-start
  115.8 3.6 collective-permute-start
  120.8 3.6 collective-permute-start
  125.9 3.6 collective-permute-start
  130.9 3.6 collective-permute-start
  136.0 3.6 collective-permute-start
  141.0 3.6 collective-permute-start
  146.1 3.6 collective-permute-start
  151.1 3.6 collective-permute-start
  156.2 3.6 collective-permute-start
  159.8 2.5 collective-permute-done
  162.3 2.5 collective-permute-start
  164.9 4.6 %collective-permute-done = f32[16,256]{1,0:T(8,128)S(1)} collective-permute-done((f32[16,256]{1,0:T(8,128)S(1)}, f32[16,256]{1,0:T(8,128)S(1)}, u32[]{:S(2)}, u32[]{:S(2)}) %collective-permute-start) | collective-permute-done | bytes 16416 | tf_op jit(solution)/shard_map/while/body/eval_jaxpr/ppermute | solution.py:10
  171.4 5.2 %collective-permute-done = f32[16,256]{1,0:T(8,128)S(1)} collective-permute-done((f32[16,256]{1,0:T(8,128)S(1)}, f32[16,256]{1,0:T(8,128)S(1)}, u32[]{:S(2)}, u32[]{:S(2)}) %collective-permute-start) | collective-permute-done | bytes 16416 | tf_op jit(solution)/shard_map/while/body/eval_jaxpr/ppermute | solution.py:10
  178.6 5.2 %collective-permute-done = f32[16,256]{1,0:T(8,128)S(1)} collective-permute-done((f32[16,256]{1,0:T(8,128)S(1)}, f32[16,256]{1,0:T(8,128)S(1)}, u32[]{:S(2)}, u32[]{:S(2)}) %collective-permute-start) | collective-permute-done | bytes 16416 | tf_op jit(solution)/shard_map/while/body/eval_jaxpr/ppermute | solution.py:10
  185.7 5.2 %collective-permute-done = f32[16,256]{1,0:T(8,128)S(1)} collective-permute-done((f32[16,256]{1,0:T(8,128)S(1)}, f32[16,256]{1,0:T(8,128)S(1)}, u32[]{:S(2)}, u32[]{:S(2)}) %collective-permute-start) | collective-permute-done | bytes 16416 | tf_op jit(solution)/shard_map/while/body/eval_jaxpr/ppermute | solution.py:10
  192.9 5.2 %collective-permute-done = f32[16,256]{1,0:T(8,128)S(1)} collective-permute-done((f32[16,256]{1,0:T(8,128)S(1)}, f32[16,256]{1,0:T(8,128)S(1)}, u32[]{:S(2)}, u32[]{:S(2)}) %collective-permute-start) | collective-permute-done | bytes 16416 | tf_op jit(solution)/shard_map/while/body/eval_jaxpr/ppermute | solution.py:10
  198.2 4.9 %multiply_reduce_fusion = f32[2,128,256]{1,2,0:T(8,128)S(1)} fusion(f32[2,128,16,256]{1,3,2,0:T(8,128)} %bitcast.72, f32[2,16,256]{2,1,0:T(8,128)S(1)} %multiply_add_fusion.2, f32[128,16,256]{0,2,1:T(8,128)} %get-tuple-element.58, f32[128,16,256]{0,2,1:T(8,128)} %get-tuple-element.59, f32[16,256]{1,0:T(8,128)S(1)} %copy-done.5), kind=kLoop, calls=%fused_computation.9 | loop fusion | flops 5177344 | bytes 8699904 | tf_op jit(solution)/shard_map/reduce_sum | solution.py:67
  203.3 1.9 collective-permute-start.1
  205.3 5.2 %collective-permute-done.1 = f32[3,2,256]{2,1,0:T(2,128)S(1)} collective-permute-done((f32[3,2,256]{2,1,0:T(2,128)S(1)}, f32[3,2,256]{2,1,0:T(2,128)S(1)}, u32[]{:S(2)}, u32[]{:S(2)}) %collective-permute-start.1) | collective-permute-done | bytes 6176 | tf_op jit(solution)/shard_map/ppermute | solution.py:10
  210.6 6.0 %fusion.1 = bf16[4096,256]{0,1:T(8,128)(2,1)} fusion(bf16[3,4096,256]{2,1,0:T(8,128)(2,1)} %param.14, f32[3,258,256]{2,1,0:T(8,128)S(1)} %pad_maximum_fusion, f32[3,256]{1,0:T(4,128)S(1)} %get-tuple-element.60, f32[3,256]{1,0:T(4,128)S(1)} %get-tuple-element.61, f32[3,256]{1,0:T(4,128)S(1)} %bitcast.84, f32[1,256,256]{2,1,0:T(8,128)S(1)} %get-tuple-element.42, ...), kind=kOutput, calls=%fused_computation.3 | convolution fusion | flops 1613234176 | bytes 10760192 | tf_op jit(solution)/shard_map/jdc,jtc->dt/dot_general | solution.py:79
  218.7 4.4 fusion.2
  223.1 63.4 %psum.7 = f32[16,256]{1,0:T(8,128)S(1)} all-reduce(f32[16,256]{1,0:T(8,128)S(1)} %reduce_sum.35), channel_id=1, replica_groups=mesh['ctx'=16,'chan'=16] {'ctx'}, use_global_device_ids=true, to_apply=%region_6.7 | all-reduce | flops 4096 | bytes 32768 | tf_op jit(solution)/shard_map/psum | solution.py:86
  287.1 154.8 %reduce-scatter.2.cloned.1.call-done = bf16[256,256]{0,1:T(8,128)(2,1)} async-done(((bf16[4096,256]{0,1:T(8,128)(2,1)}), bf16[256,256]{0,1:T(8,128)(2,1)}) %reduce-scatter.2.cloned.1.call-update) | async-done | bytes 131088 | tf_op jit(solution)/shard_map/reduce_scatter | solution.py:78
  (75 shorter events, 32.3 us)
Async XLA Ops:
  7.2 90.9 %copy-start = (bf16[256,4096]{1,0:T(8,128)(2,1)S(1)}, bf16[256,4096]{1,0:T(8,128)(2,1)}, u32[]{:S(2)}) copy-start(bf16[256,4096]{1,0:T(8,128)(2,1)} %param.13) | copy-start | bytes 6291460
  7.2 90.9 %all-gather.2.cloned.1.call-start = ((), (), s32[]{:S(2)}) async-start(), calls=%async_computation.1 | async-start | bytes 2228224 | tf_op jit(solution)/shard_map/all_gather | solution.py:25
  7.9 434.0 %reduce-scatter.2.cloned.1.call-start = ((), (), s32[]{:S(2)}) async-start(), calls=%async_computation.2 | async-start | bytes 2228224 | tf_op jit(solution)/shard_map/reduce_scatter | solution.py:78
  12.7 85.3 %copy-start.2 = (bf16[3,256,256]{2,1,0:T(8,128)(2,1)S(1)}, bf16[3,256,256]{2,1,0:T(8,128)(2,1)}, u32[]{:S(2)}) copy-start(bf16[3,256,256]{2,1,0:T(8,128)(2,1)} %param.10) | copy-start | bytes 1179652
  12.7 85.3 %copy-start.3 = (bf16[256,256]{1,0:T(8,128)(2,1)S(1)}, bf16[256,256]{1,0:T(8,128)(2,1)}, u32[]{:S(2)}) copy-start(bf16[256,256]{1,0:T(8,128)(2,1)} %param.11) | copy-start | bytes 393220
  104.5 2.6 copy-start.1
  110.0 2.3 copy-start.4
  110.0 88.2 %copy-start.5 = (f32[16,256]{1,0:T(8,128)S(1)}, f32[16,256]{1,0:T(8,128)}, u32[]{:S(2)}) copy-start(f32[16,256]{1,0:T(8,128)} %param.16) | copy-start | bytes 49156
  112.4 3.4 collective-permute-start
  115.8 5.0 %collective-permute-start = (f32[16,256]{1,0:T(8,128)S(1)}, f32[16,256]{1,0:T(8,128)S(1)}, u32[]{:S(2)}, u32[]{:S(2)}) collective-permute-start(f32[16,256]{1,0:T(8,128)S(1)} %multiply_add_fusion.4), channel_id=1, source_target_pairs={{16,0},{32,16},{48,32},{64,48},{80,64},{96,80},{112,96},{128,112},... | collective-permute-start | bytes 49160 | tf_op jit(solution)/shard_map/while/body/eval_jaxpr/ppermute | solution.py:10
  120.8 5.0 %collective-permute-start = (f32[16,256]{1,0:T(8,128)S(1)}, f32[16,256]{1,0:T(8,128)S(1)}, u32[]{:S(2)}, u32[]{:S(2)}) collective-permute-start(f32[16,256]{1,0:T(8,128)S(1)} %multiply_add_fusion.4), channel_id=1, source_target_pairs={{16,0},{32,16},{48,32},{64,48},{80,64},{96,80},{112,96},{128,112},... | collective-permute-start | bytes 49160 | tf_op jit(solution)/shard_map/while/body/eval_jaxpr/ppermute | solution.py:10
  125.9 5.0 %collective-permute-start = (f32[16,256]{1,0:T(8,128)S(1)}, f32[16,256]{1,0:T(8,128)S(1)}, u32[]{:S(2)}, u32[]{:S(2)}) collective-permute-start(f32[16,256]{1,0:T(8,128)S(1)} %multiply_add_fusion.4), channel_id=1, source_target_pairs={{16,0},{32,16},{48,32},{64,48},{80,64},{96,80},{112,96},{128,112},... | collective-permute-start | bytes 49160 | tf_op jit(solution)/shard_map/while/body/eval_jaxpr/ppermute | solution.py:10
  130.9 5.0 %collective-permute-start = (f32[16,256]{1,0:T(8,128)S(1)}, f32[16,256]{1,0:T(8,128)S(1)}, u32[]{:S(2)}, u32[]{:S(2)}) collective-permute-start(f32[16,256]{1,0:T(8,128)S(1)} %multiply_add_fusion.4), channel_id=1, source_target_pairs={{16,0},{32,16},{48,32},{64,48},{80,64},{96,80},{112,96},{128,112},... | collective-permute-start | bytes 49160 | tf_op jit(solution)/shard_map/while/body/eval_jaxpr/ppermute | solution.py:10
  136.0 5.0 %collective-permute-start = (f32[16,256]{1,0:T(8,128)S(1)}, f32[16,256]{1,0:T(8,128)S(1)}, u32[]{:S(2)}, u32[]{:S(2)}) collective-permute-start(f32[16,256]{1,0:T(8,128)S(1)} %multiply_add_fusion.4), channel_id=1, source_target_pairs={{16,0},{32,16},{48,32},{64,48},{80,64},{96,80},{112,96},{128,112},... | collective-permute-start | bytes 49160 | tf_op jit(solution)/shard_map/while/body/eval_jaxpr/ppermute | solution.py:10
  141.0 5.0 %collective-permute-start = (f32[16,256]{1,0:T(8,128)S(1)}, f32[16,256]{1,0:T(8,128)S(1)}, u32[]{:S(2)}, u32[]{:S(2)}) collective-permute-start(f32[16,256]{1,0:T(8,128)S(1)} %multiply_add_fusion.4), channel_id=1, source_target_pairs={{16,0},{32,16},{48,32},{64,48},{80,64},{96,80},{112,96},{128,112},... | collective-permute-start | bytes 49160 | tf_op jit(solution)/shard_map/while/body/eval_jaxpr/ppermute | solution.py:10
  146.1 5.0 %collective-permute-start = (f32[16,256]{1,0:T(8,128)S(1)}, f32[16,256]{1,0:T(8,128)S(1)}, u32[]{:S(2)}, u32[]{:S(2)}) collective-permute-start(f32[16,256]{1,0:T(8,128)S(1)} %multiply_add_fusion.4), channel_id=1, source_target_pairs={{16,0},{32,16},{48,32},{64,48},{80,64},{96,80},{112,96},{128,112},... | collective-permute-start | bytes 49160 | tf_op jit(solution)/shard_map/while/body/eval_jaxpr/ppermute | solution.py:10
  151.1 5.0 %collective-permute-start = (f32[16,256]{1,0:T(8,128)S(1)}, f32[16,256]{1,0:T(8,128)S(1)}, u32[]{:S(2)}, u32[]{:S(2)}) collective-permute-start(f32[16,256]{1,0:T(8,128)S(1)} %multiply_add_fusion.4), channel_id=1, source_target_pairs={{16,0},{32,16},{48,32},{64,48},{80,64},{96,80},{112,96},{128,112},... | collective-permute-start | bytes 49160 | tf_op jit(solution)/shard_map/while/body/eval_jaxpr/ppermute | solution.py:10
  156.2 6.1 %collective-permute-start = (f32[16,256]{1,0:T(8,128)S(1)}, f32[16,256]{1,0:T(8,128)S(1)}, u32[]{:S(2)}, u32[]{:S(2)}) collective-permute-start(f32[16,256]{1,0:T(8,128)S(1)} %multiply_add_fusion.4), channel_id=1, source_target_pairs={{16,0},{32,16},{48,32},{64,48},{80,64},{96,80},{112,96},{128,112},... | collective-permute-start | bytes 49160 | tf_op jit(solution)/shard_map/while/body/eval_jaxpr/ppermute | solution.py:10
  162.3 7.2 %collective-permute-start = (f32[16,256]{1,0:T(8,128)S(1)}, f32[16,256]{1,0:T(8,128)S(1)}, u32[]{:S(2)}, u32[]{:S(2)}) collective-permute-start(f32[16,256]{1,0:T(8,128)S(1)} %multiply_add_fusion.4), channel_id=1, source_target_pairs={{16,0},{32,16},{48,32},{64,48},{80,64},{96,80},{112,96},{128,112},... | collective-permute-start | bytes 49160 | tf_op jit(solution)/shard_map/while/body/eval_jaxpr/ppermute | solution.py:10
  169.5 7.2 %collective-permute-start = (f32[16,256]{1,0:T(8,128)S(1)}, f32[16,256]{1,0:T(8,128)S(1)}, u32[]{:S(2)}, u32[]{:S(2)}) collective-permute-start(f32[16,256]{1,0:T(8,128)S(1)} %multiply_add_fusion.4), channel_id=1, source_target_pairs={{16,0},{32,16},{48,32},{64,48},{80,64},{96,80},{112,96},{128,112},... | collective-permute-start | bytes 49160 | tf_op jit(solution)/shard_map/while/body/eval_jaxpr/ppermute | solution.py:10
  176.6 7.2 %collective-permute-start = (f32[16,256]{1,0:T(8,128)S(1)}, f32[16,256]{1,0:T(8,128)S(1)}, u32[]{:S(2)}, u32[]{:S(2)}) collective-permute-start(f32[16,256]{1,0:T(8,128)S(1)} %multiply_add_fusion.4), channel_id=1, source_target_pairs={{16,0},{32,16},{48,32},{64,48},{80,64},{96,80},{112,96},{128,112},... | collective-permute-start | bytes 49160 | tf_op jit(solution)/shard_map/while/body/eval_jaxpr/ppermute | solution.py:10
  183.8 7.2 %collective-permute-start = (f32[16,256]{1,0:T(8,128)S(1)}, f32[16,256]{1,0:T(8,128)S(1)}, u32[]{:S(2)}, u32[]{:S(2)}) collective-permute-start(f32[16,256]{1,0:T(8,128)S(1)} %multiply_add_fusion.4), channel_id=1, source_target_pairs={{16,0},{32,16},{48,32},{64,48},{80,64},{96,80},{112,96},{128,112},... | collective-permute-start | bytes 49160 | tf_op jit(solution)/shard_map/while/body/eval_jaxpr/ppermute | solution.py:10
  191.0 7.2 %collective-permute-start = (f32[16,256]{1,0:T(8,128)S(1)}, f32[16,256]{1,0:T(8,128)S(1)}, u32[]{:S(2)}, u32[]{:S(2)}) collective-permute-start(f32[16,256]{1,0:T(8,128)S(1)} %multiply_add_fusion.4), channel_id=1, source_target_pairs={{16,0},{32,16},{48,32},{64,48},{80,64},{96,80},{112,96},{128,112},... | collective-permute-start | bytes 49160 | tf_op jit(solution)/shard_map/while/body/eval_jaxpr/ppermute | solution.py:10
  203.3 7.2 %collective-permute-start.1 = (f32[3,2,256]{2,1,0:T(2,128)S(1)}, f32[3,2,256]{2,1,0:T(2,128)S(1)}, u32[]{:S(2)}, u32[]{:S(2)}) collective-permute-start(f32[3,2,256]{2,1,0:T(2,128)S(1)} %slice.53), channel_id=1, source_target_pairs={{16,0},{32,16},{48,32},{64,48},{80,64},{96,80},{112,96},{128,112},... | collective-permute-start | bytes 18440 | tf_op jit(solution)/shard_map/ppermute | solution.py:10
Sparse Core Ops, SparseCore 0:
  10.5 87.5 all-gather.1
  216.7 225.1 reduce-scatter.1
where the time goes:
time: 451 us; the launch traced here: 450 us
  waiting for transfers between devices  285 us (63%)
  blocking collectives  63.4 us (14%)
  starting transfers between devices  46.6 us (10%)
  other arithmetic  20.2 us (4%)
  between operations  14.3 us (3%)
  local copies, waits for them, and re-layouts  10.6 us (2%)
  matrix products  10.5 us (2%)
    reduce_scatter x1, waiting for transfers between devices, local(): lax.psum_scatter(jnp.einsum('jdc,jtc->dt', in_weight, grad_proj, preferre...  155 us
    all_gather x1, waiting for transfers between devices, local(): everything = lax.all_gather(grad_out, 'chan', axis=1, tiled=True)  83 us
    psum x1, blocking collectives, local(): lax.psum(partial_res, 'ctx') / (length * lax.axis_size('ctx'))  63.4 us
    ppermute x16, starting transfers between devices, passed_along(): lax.ppermute(value, axis, [(source, source + steps) for source in range(l...  46.6 us
    ppermute x16, waiting for transfers between devices, passed_along(): lax.ppermute(value, axis, [(source, source + steps) for source in range(l...  46 us
  transfers between devices with their start and end apart: 18, of which 18 were waited for; matrix products, arithmetic and copies ran while one was open for 3% of the time, Pallas kernels for 0%

commit v1 on v0

--- a/solution.py
+++ b/solution.py
@@ -22,7 +22,9 @@
     key_act = features[1].astype(jnp.float32)
     value_act = features[2].astype(jnp.float32)
     contract = (((1,), (1,)), ((), ()))
-    everything = lax.all_gather(grad_out, "chan", axis=1, tiled=True)
+    everything = jnp.concatenate(
+        lax.all_to_all(jnp.stack([grad_out] * lax.axis_size("chan")), "chan", 0, 0), axis=1
+    )
     grad_gate = lax.dot_general(
         everything, out_weight, contract, preferred_element_type=jnp.float32
     )

time: 451 us -> 427 us (0.947)
  waiting for transfers between devices: 285 us -> 248 us
  starting transfers between devices: 46.6 us -> 57.4 us
    all_gather x1 -> x0, waiting for transfers between devices: 83 us -> none  [local(): everything = lax.all_gather(grad_out, 'chan', axis=1, tiled=True)]
    all_to_all x0 -> x1, waiting for transfers between devices: none -> 46.4 us  [local(): lax.all_to_all(jnp.stack([grad_out] * lax.axis_size('chan')), 'chan', 0, 0)]
    all_to_all x0 -> x1, starting transfers between devices: none -> 11.4 us  [local(): lax.all_to_all(jnp.stack([grad_out] * lax.axis_size('chan')), 'chan', 0, 0)]
where the time goes in v1:
time: 427 us
  waiting for transfers between devices  248 us (58%)
  blocking collectives  63.7 us (15%)
  starting transfers between devices  57.4 us (13%)
  other arithmetic  19.5 us (5%)
  between operations  14.3 us (3%)
  local copies, waits for them, and re-layouts  12.5 us (3%)
  matrix products  10.5 us (2%)
    reduce_scatter x1, waiting for transfers between devices, local(): lax.psum_scatter(jnp.einsum('jdc,jtc->dt', in_weight, grad_proj, preferre...  155 us
    psum x1, blocking collectives, local(): lax.psum(partial_res, 'ctx') / (length * lax.axis_size('ctx'))  63.7 us
    ppermute x16, waiting for transfers between devices, passed_along(): lax.ppermute(value, axis, [(source, source + steps) for source in range(l...  47.3 us
    all_to_all x1, waiting for transfers between devices, local(): lax.all_to_all(jnp.stack([grad_out] * lax.axis_size('chan')), 'chan', 0, 0)  46.4 us
    ppermute x16, starting transfers between devices, passed_along(): lax.ppermute(value, axis, [(source, source + steps) for source in range(l...  45.9 us
    all_to_all x1, starting transfers between devices, local(): lax.all_to_all(jnp.stack([grad_out] * lax.axis_size('chan')), 'chan', 0, 0)  11.4 us
    unnamed x25, local copies, waits for them, and re-layouts  8.98 us
  transfers between devices with their start and end apart: 18, of which 18 were waited for; matrix products, arithmetic and copies ran while one was open for 3% of the time, Pallas kernels for 0%

profile of v1, /device:TPU:2, one launch (start us, length us, event | category | flops | bytes accessed | tf_op | source)
XLA Modules:
  0.0 426.5 jit_solution(17996620497709196146)
XLA Ops:
  9.9 11.4 %all-to-all-start = ((bf16[16,256,256]{1,2,0:T(8,128)(2,1)}), bf16[16,256,256]{1,2,0:T(8,128)(2,1)}, u32[]{:S(2)}, u32[]{:S(2)}) async-start(bf16[16,256,256]{1,2,0:T(8,128)(2,1)} %stack.6), calls=%async_computation | async-start | bytes 4194304 | tf_op jit(solution)/shard_map/all_to_all | solution.py:26
  21.4 3.1 multiply_exponential_fusion.2
  24.5 2.4 multiply_exponential_fusion
  26.9 46.4 %all-to-all-done = bf16[16,256,256]{1,2,0:T(8,128)(2,1)} async-done(((bf16[16,256,256]{1,2,0:T(8,128)(2,1)}), bf16[16,256,256]{1,2,0:T(8,128)(2,1)}, u32[]{:S(2)}, u32[]{:S(2)}) %all-to-all-start) | async-done | bytes 2097184 | tf_op jit(solution)/shard_map/all_to_all | solution.py:26
  73.3 2.3 multiply_bitcast_fusion
  77.7 2.1 fusion.12
  82.4 2.8 copy.37
  85.3 2.2 copy.38
  87.6 86.4 %while.10 = (s32[]{:T(128)}, f32[16,256]{1,0:T(8,128)S(1)}, f32[16,256]{1,0:T(8,128)S(1)}, f32[16,256]{1,0:T(8,128)S(1)}, s32[]{:T(128)}) while((s32[]{:T(128)}, f32[16,256]{1,0:T(8,128)S(1)}, f32[16,256]{1,0:T(8,128)S(1)}, f32[16,256]{1,0:T(8,128)S(1)}, s32[]{:T(128)}) %tuple.40), condition=%wide.region_2.3_spmd, body=%wide.region_1.2_spmd.sunk | while | flops 8194 | bytes 131173 | solution.py:65
  87.6 1.9 collective-permute-start
  91.0 3.6 collective-permute-start
  96.1 3.6 collective-permute-start
  101.1 3.6 collective-permute-start
  106.2 3.6 collective-permute-start
  111.2 3.6 collective-permute-start
  116.3 3.6 collective-permute-start
  121.3 3.6 collective-permute-start
  126.4 3.6 collective-permute-start
  131.4 3.6 collective-permute-start
  135.1 3.2 collective-permute-done
  140.2 5.2 %collective-permute-done = f32[16,256]{1,0:T(8,128)S(1)} collective-permute-done((f32[16,256]{1,0:T(8,128)S(1)}, f32[16,256]{1,0:T(8,128)S(1)}, u32[]{:S(2)}, u32[]{:S(2)}) %collective-permute-start) | collective-permute-done | bytes 16416 | tf_op jit(solution)/shard_map/while/body/eval_jaxpr/ppermute | solution.py:10
  147.3 5.2 %collective-permute-done = f32[16,256]{1,0:T(8,128)S(1)} collective-permute-done((f32[16,256]{1,0:T(8,128)S(1)}, f32[16,256]{1,0:T(8,128)S(1)}, u32[]{:S(2)}, u32[]{:S(2)}) %collective-permute-start) | collective-permute-done | bytes 16416 | tf_op jit(solution)/shard_map/while/body/eval_jaxpr/ppermute | solution.py:10
  154.5 5.2 %collective-permute-done = f32[16,256]{1,0:T(8,128)S(1)} collective-permute-done((f32[16,256]{1,0:T(8,128)S(1)}, f32[16,256]{1,0:T(8,128)S(1)}, u32[]{:S(2)}, u32[]{:S(2)}) %collective-permute-start) | collective-permute-done | bytes 16416 | tf_op jit(solution)/shard_map/while/body/eval_jaxpr/ppermute | solution.py:10
  161.6 5.2 %collective-permute-done = f32[16,256]{1,0:T(8,128)S(1)} collective-permute-done((f32[16,256]{1,0:T(8,128)S(1)}, f32[16,256]{1,0:T(8,128)S(1)}, u32[]{:S(2)}, u32[]{:S(2)}) %collective-permute-start) | collective-permute-done | bytes 16416 | tf_op jit(solution)/shard_map/while/body/eval_jaxpr/ppermute | solution.py:10
  168.8 5.2 %collective-permute-done = f32[16,256]{1,0:T(8,128)S(1)} collective-permute-done((f32[16,256]{1,0:T(8,128)S(1)}, f32[16,256]{1,0:T(8,128)S(1)}, u32[]{:S(2)}, u32[]{:S(2)}) %collective-permute-start) | collective-permute-done | bytes 16416 | tf_op jit(solution)/shard_map/while/body/eval_jaxpr/ppermute | solution.py:10
  174.1 4.9 %multiply_reduce_fusion = f32[2,128,256]{1,2,0:T(8,128)S(1)} fusion(f32[2,128,16,256]{1,3,2,0:T(8,128)} %bitcast.75, f32[2,16,256]{2,1,0:T(8,128)S(1)} %multiply_add_fusion.2, f32[128,16,256]{0,2,1:T(8,128)} %get-tuple-element.58, f32[128,16,256]{0,2,1:T(8,128)} %get-tuple-element.59, f32[16,256]{1,0:T(8,128)S(1)} %copy-done.5), kind=kLoop, calls=%fused_computation.9 | loop fusion | flops 5177344 | bytes 8699904 | tf_op jit(solution)/shard_map/reduce_sum | solution.py:69
  179.3 1.9 collective-permute-start.1
  181.2 5.2 %collective-permute-done.1 = f32[3,2,256]{2,1,0:T(2,128)S(1)} collective-permute-done((f32[3,2,256]{2,1,0:T(2,128)S(1)}, f32[3,2,256]{2,1,0:T(2,128)S(1)}, u32[]{:S(2)}, u32[]{:S(2)}) %collective-permute-start.1) | collective-permute-done | bytes 6176 | tf_op jit(solution)/shard_map/ppermute | solution.py:10
  186.5 6.0 %fusion.1 = bf16[4096,256]{0,1:T(8,128)(2,1)} fusion(bf16[3,4096,256]{2,1,0:T(8,128)(2,1)} %param.14, f32[3,258,256]{2,1,0:T(8,128)S(1)} %pad_maximum_fusion, f32[3,256]{1,0:T(4,128)S(1)} %get-tuple-element.60, f32[3,256]{1,0:T(4,128)S(1)} %get-tuple-element.61, f32[3,256]{1,0:T(4,128)S(1)} %bitcast.87, f32[1,256,256]{2,1,0:T(8,128)S(1)} %get-tuple-element.42, ...), kind=kOutput, calls=%fused_computation.3 | convolution fusion | flops 1613234176 | bytes 10760192 | tf_op jit(solution)/shard_map/jdc,jtc->dt/dot_general | solution.py:81
  194.6 4.4 %fusion.2 = f32[4096]{0:T(1024)S(1)} fusion(f32[2,4096,128]{2,1,0:T(8,128)} %copy-done.1, f32[2,4096]{1,0:T(2,128)S(1)} %multiply_add_fusion.1, f32[128,4096]{0,1:T(8,128)} %get-tuple-element.53, f32[128,4096]{0,1:T(8,128)} %multiply_exponential_fusion.1, f32[2,128,256]{1,2,0:T(8,128)S(1)} %copy.32), kind=kLoop, calls=%fused_computation.5 | loop fusion | flops 5238784 | bytes 8699904 | tf_op jit(solution)/shard_map/reduce_sum | solution.py:70
  199.0 63.7 %psum.7 = f32[16,256]{1,0:T(8,128)S(1)} all-reduce(f32[16,256]{1,0:T(8,128)S(1)} %reduce_sum.35), channel_id=1, replica_groups=mesh['ctx'=16,'chan'=16] {'ctx'}, use_global_device_ids=true, to_apply=%region_6.7 | all-reduce | flops 4096 | bytes 32768 | tf_op jit(solution)/shard_map/psum | solution.py:88
  263.3 154.7 %reduce-scatter.2.cloned.1.call-done = bf16[256,256]{0,1:T(8,128)(2,1)} async-done(((bf16[4096,256]{0,1:T(8,128)(2,1)}), bf16[256,256]{0,1:T(8,128)(2,1)}) %reduce-scatter.2.cloned.1.call-update) | async-done | bytes 131088 | tf_op jit(solution)/shard_map/reduce_scatter | solution.py:80
  (78 shorter events, 34.6 us)
Async XLA Ops:
  7.2 66.1 %copy-start = (bf16[256,4096]{1,0:T(8,128)(2,1)S(1)}, bf16[256,4096]{1,0:T(8,128)(2,1)}, u32[]{:S(2)}) copy-start(bf16[256,4096]{1,0:T(8,128)(2,1)} %param.13) | copy-start | bytes 6291460
  9.8 11.4 %copy-start.4 = (f32[16,256]{1,0:T(8,128)S(1)}, f32[16,256]{1,0:T(8,128)}, u32[]{:S(2)}) copy-start(f32[16,256]{1,0:T(8,128)} %param.17) | copy-start | bytes 49156
  9.9 11.5 %copy-start.6 = (f32[3,3,256]{2,1,0:T(4,128)S(1)}, f32[3,3,256]{2,1,0:T(4,128)}, u32[]{:S(2)}) copy-start(f32[3,3,256]{2,1,0:T(4,128)} %param.15) | copy-start | bytes 27652
  9.9 63.5 %all-to-all-start = ((bf16[16,256,256]{1,2,0:T(8,128)(2,1)}), bf16[16,256,256]{1,2,0:T(8,128)(2,1)}, u32[]{:S(2)}, u32[]{:S(2)}) async-start(bf16[16,256,256]{1,2,0:T(8,128)(2,1)} %stack.6), calls=%async_computation | async-start | bytes 4194304 | tf_op jit(solution)/shard_map/all_to_all | solution.py:26
  21.2 396.8 %reduce-scatter.2.cloned.1.call-start = ((), (), s32[]{:S(2)}) async-start(), calls=%async_computation.2 | async-start | bytes 2228224 | tf_op jit(solution)/shard_map/reduce_scatter | solution.py:80
  24.5 48.8 %copy-start.2 = (bf16[3,256,256]{2,1,0:T(8,128)(2,1)S(1)}, bf16[3,256,256]{2,1,0:T(8,128)(2,1)}, u32[]{:S(2)}) copy-start(bf16[3,256,256]{2,1,0:T(8,128)(2,1)} %param.10) | copy-start | bytes 1179652
  24.5 48.8 %copy-start.3 = (bf16[256,256]{1,0:T(8,128)(2,1)S(1)}, bf16[256,256]{1,0:T(8,128)(2,1)}, u32[]{:S(2)}) copy-start(bf16[256,256]{1,0:T(8,128)(2,1)} %param.11) | copy-start | bytes 393220
  79.8 2.6 copy-start.1
  85.3 88.9 %copy-start.5 = (f32[16,256]{1,0:T(8,128)S(1)}, f32[16,256]{1,0:T(8,128)}, u32[]{:S(2)}) copy-start(f32[16,256]{1,0:T(8,128)} %param.16) | copy-start | bytes 49156
  87.6 3.4 collective-permute-start
  91.0 5.0 %collective-permute-start = (f32[16,256]{1,0:T(8,128)S(1)}, f32[16,256]{1,0:T(8,128)S(1)}, u32[]{:S(2)}, u32[]{:S(2)}) collective-permute-start(f32[16,256]{1,0:T(8,128)S(1)} %multiply_add_fusion.4), channel_id=1, source_target_pairs={{16,0},{32,16},{48,32},{64,48},{80,64},{96,80},{112,96},{128,112},... | collective-permute-start | bytes 49160 | tf_op jit(solution)/shard_map/while/body/eval_jaxpr/ppermute | solution.py:10
  96.1 5.0 %collective-permute-start = (f32[16,256]{1,0:T(8,128)S(1)}, f32[16,256]{1,0:T(8,128)S(1)}, u32[]{:S(2)}, u32[]{:S(2)}) collective-permute-start(f32[16,256]{1,0:T(8,128)S(1)} %multiply_add_fusion.4), channel_id=1, source_target_pairs={{16,0},{32,16},{48,32},{64,48},{80,64},{96,80},{112,96},{128,112},... | collective-permute-start | bytes 49160 | tf_op jit(solution)/shard_map/while/body/eval_jaxpr/ppermute | solution.py:10
  101.1 5.0 %collective-permute-start = (f32[16,256]{1,0:T(8,128)S(1)}, f32[16,256]{1,0:T(8,128)S(1)}, u32[]{:S(2)}, u32[]{:S(2)}) collective-permute-start(f32[16,256]{1,0:T(8,128)S(1)} %multiply_add_fusion.4), channel_id=1, source_target_pairs={{16,0},{32,16},{48,32},{64,48},{80,64},{96,80},{112,96},{128,112},... | collective-permute-start | bytes 49160 | tf_op jit(solution)/shard_map/while/body/eval_jaxpr/ppermute | solution.py:10
  106.2 5.0 %collective-permute-start = (f32[16,256]{1,0:T(8,128)S(1)}, f32[16,256]{1,0:T(8,128)S(1)}, u32[]{:S(2)}, u32[]{:S(2)}) collective-permute-start(f32[16,256]{1,0:T(8,128)S(1)} %multiply_add_fusion.4), channel_id=1, source_target_pairs={{16,0},{32,16},{48,32},{64,48},{80,64},{96,80},{112,96},{128,112},... | collective-permute-start | bytes 49160 | tf_op jit(solution)/shard_map/while/body/eval_jaxpr/ppermute | solution.py:10
  111.2 5.0 %collective-permute-start = (f32[16,256]{1,0:T(8,128)S(1)}, f32[16,256]{1,0:T(8,128)S(1)}, u32[]{:S(2)}, u32[]{:S(2)}) collective-permute-start(f32[16,256]{1,0:T(8,128)S(1)} %multiply_add_fusion.4), channel_id=1, source_target_pairs={{16,0},{32,16},{48,32},{64,48},{80,64},{96,80},{112,96},{128,112},... | collective-permute-start | bytes 49160 | tf_op jit(solution)/shard_map/while/body/eval_jaxpr/ppermute | solution.py:10
  116.3 5.0 %collective-permute-start = (f32[16,256]{1,0:T(8,128)S(1)}, f32[16,256]{1,0:T(8,128)S(1)}, u32[]{:S(2)}, u32[]{:S(2)}) collective-permute-start(f32[16,256]{1,0:T(8,128)S(1)} %multiply_add_fusion.4), channel_id=1, source_target_pairs={{16,0},{32,16},{48,32},{64,48},{80,64},{96,80},{112,96},{128,112},... | collective-permute-start | bytes 49160 | tf_op jit(solution)/shard_map/while/body/eval_jaxpr/ppermute | solution.py:10
  121.3 5.0 %collective-permute-start = (f32[16,256]{1,0:T(8,128)S(1)}, f32[16,256]{1,0:T(8,128)S(1)}, u32[]{:S(2)}, u32[]{:S(2)}) collective-permute-start(f32[16,256]{1,0:T(8,128)S(1)} %multiply_add_fusion.4), channel_id=1, source_target_pairs={{16,0},{32,16},{48,32},{64,48},{80,64},{96,80},{112,96},{128,112},... | collective-permute-start | bytes 49160 | tf_op jit(solution)/shard_map/while/body/eval_jaxpr/ppermute | solution.py:10
  126.4 5.0 %collective-permute-start = (f32[16,256]{1,0:T(8,128)S(1)}, f32[16,256]{1,0:T(8,128)S(1)}, u32[]{:S(2)}, u32[]{:S(2)}) collective-permute-start(f32[16,256]{1,0:T(8,128)S(1)} %multiply_add_fusion.4), channel_id=1, source_target_pairs={{16,0},{32,16},{48,32},{64,48},{80,64},{96,80},{112,96},{128,112},... | collective-permute-start | bytes 49160 | tf_op jit(solution)/shard_map/while/body/eval_jaxpr/ppermute | solution.py:10
  131.4 6.8 %collective-permute-start = (f32[16,256]{1,0:T(8,128)S(1)}, f32[16,256]{1,0:T(8,128)S(1)}, u32[]{:S(2)}, u32[]{:S(2)}) collective-permute-start(f32[16,256]{1,0:T(8,128)S(1)} %multiply_add_fusion.4), channel_id=1, source_target_pairs={{16,0},{32,16},{48,32},{64,48},{80,64},{96,80},{112,96},{128,112},... | collective-permute-start | bytes 49160 | tf_op jit(solution)/shard_map/while/body/eval_jaxpr/ppermute | solution.py:10
  138.2 7.2 %collective-permute-start = (f32[16,256]{1,0:T(8,128)S(1)}, f32[16,256]{1,0:T(8,128)S(1)}, u32[]{:S(2)}, u32[]{:S(2)}) collective-permute-start(f32[16,256]{1,0:T(8,128)S(1)} %multiply_add_fusion.4), channel_id=1, source_target_pairs={{16,0},{32,16},{48,32},{64,48},{80,64},{96,80},{112,96},{128,112},... | collective-permute-start | bytes 49160 | tf_op jit(solution)/shard_map/while/body/eval_jaxpr/ppermute | solution.py:10
  145.4 7.2 %collective-permute-start = (f32[16,256]{1,0:T(8,128)S(1)}, f32[16,256]{1,0:T(8,128)S(1)}, u32[]{:S(2)}, u32[]{:S(2)}) collective-permute-start(f32[16,256]{1,0:T(8,128)S(1)} %multiply_add_fusion.4), channel_id=1, source_target_pairs={{16,0},{32,16},{48,32},{64,48},{80,64},{96,80},{112,96},{128,112},... | collective-permute-start | bytes 49160 | tf_op jit(solution)/shard_map/while/body/eval_jaxpr/ppermute | solution.py:10
  152.6 7.2 %collective-permute-start = (f32[16,256]{1,0:T(8,128)S(1)}, f32[16,256]{1,0:T(8,128)S(1)}, u32[]{:S(2)}, u32[]{:S(2)}) collective-permute-start(f32[16,256]{1,0:T(8,128)S(1)} %multiply_add_fusion.4), channel_id=1, source_target_pairs={{16,0},{32,16},{48,32},{64,48},{80,64},{96,80},{112,96},{128,112},... | collective-permute-start | bytes 49160 | tf_op jit(solution)/shard_map/while/body/eval_jaxpr/ppermute | solution.py:10
  159.7 7.2 %collective-permute-start = (f32[16,256]{1,0:T(8,128)S(1)}, f32[16,256]{1,0:T(8,128)S(1)}, u32[]{:S(2)}, u32[]{:S(2)}) collective-permute-start(f32[16,256]{1,0:T(8,128)S(1)} %multiply_add_fusion.4), channel_id=1, source_target_pairs={{16,0},{32,16},{48,32},{64,48},{80,64},{96,80},{112,96},{128,112},... | collective-permute-start | bytes 49160 | tf_op jit(solution)/shard_map/while/body/eval_jaxpr/ppermute | solution.py:10
  166.9 7.2 %collective-permute-start = (f32[16,256]{1,0:T(8,128)S(1)}, f32[16,256]{1,0:T(8,128)S(1)}, u32[]{:S(2)}, u32[]{:S(2)}) collective-permute-start(f32[16,256]{1,0:T(8,128)S(1)} %multiply_add_fusion.4), channel_id=1, source_target_pairs={{16,0},{32,16},{48,32},{64,48},{80,64},{96,80},{112,96},{128,112},... | collective-permute-start | bytes 49160 | tf_op jit(solution)/shard_map/while/body/eval_jaxpr/ppermute | solution.py:10
  179.3 7.2 %collective-permute-start.1 = (f32[3,2,256]{2,1,0:T(2,128)S(1)}, f32[3,2,256]{2,1,0:T(2,128)S(1)}, u32[]{:S(2)}, u32[]{:S(2)}) collective-permute-start(f32[3,2,256]{2,1,0:T(2,128)S(1)} %slice.53), channel_id=1, source_target_pairs={{16,0},{32,16},{48,32},{64,48},{80,64},{96,80},{112,96},{128,112},... | collective-permute-start | bytes 18440 | tf_op jit(solution)/shard_map/ppermute | solution.py:10
Sparse Core Ops, SparseCore 0:
  192.7 225.2 reduce-scatter.1
